TPU v7x, 128 devices: a whole 4x4x4 slice. The times are simulated.
128 devices in a mesh: freq: 8 (over z, core), rcv: 16 (over x, y).
Axes of the slice: x: 4, y: 4, z: 4, core: 2. Of those that a mesh axis runs over, the one named last changes fastest.
Arguments:
- spectra: float32 [128, 2, 512, 512], P('freq', None, 'rcv'), may hold values from -0.5 to 0.5
- counts: int32 [8], replicated, may hold values from 1 to 16, 64 in all
- partner: int32 [512], replicated, may hold values from 0 to 511, as said below
- recorded: float32 [512, 512, 512], P('freq', 'rcv'), may hold values from -3 to 3
- gain_index: int32 [512, 512], P('freq', 'rcv'), may hold values from 0 to 15
- gain_table: float32 [2, 16], replicated, may hold values from 0.5 to 1.5
Outputs:
- primaries: float32 [512, 512, 512], P('freq', 'rcv')
Inputs may be any that keep to these rules, and one draw needn't show every extreme that they name: `counts`: the bands hold 64 frequencies together, and some band holds exactly 16. `partner`: A permutation that maps each aligned block of 32 indices onto itself.
All inputs are finite; a program needn't handle non-finite values.
Results may differ from a plain program's by a relative error of at most 0.00005.
Values sent between devices are 32-bit elements; how exact they have to be, the bound alone decides.
A program may use at most 128 MiB of HBM per device.

v0:
```python
import itertools

import jax
import jax.numpy as jnp
import numpy as np
from jax import lax
from jax.experimental import pallas as pl
from jax.experimental.pallas import tpu as pltpu
from jax.sharding import PartitionSpec as P

MESH = pl.DeviceIdType.MESH
ANY = pl.BlockSpec(memory_space=pl.ANY)
VMEM = pl.BlockSpec(memory_space=pltpu.VMEM)
SMEM = pl.BlockSpec(memory_space=pltpu.SMEM)

NT = 512
SIDE = 512
LIVE = 64
NP = 8
NQ = 16
F32 = jnp.float32
BF16 = jnp.bfloat16


def basis():
    bins = np.arange(1, LIVE + 1, dtype=np.int64)[:, None]
    angles = 2.0 * np.pi / NT * ((bins * np.arange(NT, dtype=np.int64)[None, :]) % NT)
    table = np.concatenate([np.cos(angles), -np.sin(angles)], axis=0).astype(np.float32)
    high = table.astype(BF16)
    low = (table - high.astype(np.float32)).astype(BF16)
    return np.concatenate([high, high, low], axis=0)


def halves(x):
    high = x.astype(BF16)
    return high, (x - high.astype(F32)).astype(BF16)


def lane_group():
    return lax.broadcasted_iota(jnp.int32, (16, 128), 1) // 32


def swap_groups(blocks, group):
    outs = []
    for g in range(4):
        out = blocks[g]
        for u in range(4):
            if u != g:
                moved = pltpu.roll(blocks[u], (32 * (u - g)) % 128, 1)
                out = jnp.where(group == u, moved, out)
        outs.append(out)
    return outs


def nt(a, b):
    return lax.dot_general(a, b, (((1,), (1,)), ((), ())), preferred_element_type=F32)


def nn(a, b):
    return jnp.dot(a, b, preferred_element_type=F32)


def look_up(index, entries):
    level = entries
    for bit in range(4):
        odd = (index & (1 << bit)) != 0
        level = [jnp.where(odd, level[2 * k + 1], level[2 * k]) for k in range(len(level) // 2)]
    return level[0]


def each(first, last, fn):
    def body(t, _):
        fn(t)
        return 0

    lax.fori_loop(first, last, body, 0)


def away(a, code):
    return a + code * (4 - 2 * a)


def ways(a):
    return 2 if a == 1 else 1


def far_first(ranges):
    return sorted(itertools.product(range(3), repeat=ranges), key=lambda c: (-sum(c), c))


def slot_kernel(
    spec, gtile, prow, tab, recv,
    whole, gains, ct, index, mirror, gain, mgain, d, direct, refl, both, send,
    own_sem, row_send, row_recv, tile_send, tile_recv, slab_send, slab_recv, turn_sem, ready_sem,
    out_own, out_send, out_recv,
):
    p, q = lax.axis_index("freq"), lax.axis_index("rcv")
    me = p * NQ + q
    z, core = p // 2, lax.rem(p, 2)
    x, y = q // 4, lax.rem(q, 4)
    mate = p + 1 - 2 * core

    barrier = pltpu.get_barrier_semaphore()

    def greet_q(t):
        pl.semaphore_signal(barrier, inc=1, device_id=(p, lax.rem(q + t, NQ)), device_id_type=MESH)

    def greet_p(t):
        pl.semaphore_signal(barrier, inc=1, device_id=(lax.rem(p + t, NP), q), device_id_type=MESH)

    each(1, NQ, greet_q)
    each(1, NP, greet_p)
    own_tile = pltpu.make_async_copy(gtile, gains.at[p, q], own_sem.at[0])
    own_rows = pltpu.make_async_copy(spec.at[q], whole.at[:, pl.ds(pl.multiple_of(q * 32, 32), 32), :], own_sem.at[1])
    own_tile.start()
    own_rows.start()
    for b in range(2):
        rows = lax.broadcasted_iota(jnp.int32, (256, 256), 0) + 256 * b
        ct[b] = (rows == prow[:, 256 * b : 256 * b + 256]).astype(F32).T.astype(BF16)
    pl.semaphore_wait(barrier, NQ + NP - 2)
    each(1, NP, lambda t: pl.semaphore_signal(
        ready_sem, inc=1, device_id=(lax.rem(p + t, NP), q), device_id_type=MESH))

    def tile(t):
        return pltpu.make_async_remote_copy(
            gtile, gains.at[p, q], tile_send.at[t], tile_recv.at[t],
            device_id=(p, lax.rem(q + t, NQ)), device_id_type=MESH)

    def row(t):
        k = lax.rem(q + t, NQ)
        return pltpu.make_async_remote_copy(
            spec.at[k], whole.at[:, pl.ds(pl.multiple_of(q * 32, 32), 32), :], row_send.at[t], row_recv.at[t],
            device_id=(p, k), device_id_type=MESH)

    def slab(k, target, t):
        return pltpu.make_async_remote_copy(
            gains.at[k], gains.at[k], slab_send.at[t], slab_recv.at[k],
            device_id=(target, q), device_id_type=MESH)

    each(1, NQ, lambda t: tile(t).start())

    @pl.when(core == 0)
    def _():
        each(1, NQ, lambda t: row(t).start())

    own_tile.wait()
    each(1, NQ, lambda t: tile(t).wait())

    each(1, 4, lambda t: slab(p, lax.rem(z + t, 4) * 2, t).start())

    @pl.when(core == 1)
    def _():
        slab(p, p - 1, 0).start()

    @pl.when(core == 0)
    def _():
        each(1, NP, lambda t: slab(lax.rem(p + t, NP), 0, 0).wait_recv())
        each(1, NP, lambda t: slab(lax.rem(p + 1 + t, NP), p + 1, t + 3).start())
        each(1, NQ, lambda t: row(t).wait_send())
        pl.semaphore_signal(turn_sem, inc=1, device_id=(p + 1, q), device_id_type=MESH)

    @pl.when(core == 1)
    def _():
        pl.semaphore_wait(turn_sem, 1)
        each(1, NQ, lambda t: row(t).start())
        each(1, NP, lambda t: slab(lax.rem(p + t, NP), 0, 0).wait_recv())

    group = lane_group()

    def place(k):
        for h in range(4):
            outs = swap_groups([gains[k, 4 * h + u] for u in range(4)], group)
            for g in range(4):
                index[h, pl.ds(k * 64 + g, 16, stride=4), :] = outs[g]

    each(0, NP, place)
    for a in range(2):
        for b in range(2):
            block = jnp.concatenate([index[2 * a + h, 256 * b : 256 * b + 256, :] for h in range(2)], axis=1).astype(F32).astype(BF16)
            moved = nt(ct[a], block).astype(BF16)
            mirror[256 * a : 256 * a + 256, 256 * b : 256 * b + 256] = nn(moved, ct[b]).astype(jnp.int32)

    def gains_of(i):
        rows = pl.ds(pl.multiple_of(i * 16, 16), 16)
        for o in range(2):
            entries = [0.5 * tab[o, k] for k in range(16)]
            for h in range(4):
                gain[o, rows, 128 * h : 128 * h + 128] = look_up(index[h, rows, :], entries)
            mgain[o, rows, :] = look_up(mirror[rows, :], entries)

    each(0, SIDE // 16, gains_of)
    own_rows.wait()
    each(1, NQ, lambda t: row(t).wait_recv())

    @pl.when(core == 1)
    def _():
        each(1, NQ, lambda t: row(t).wait_send())

    def turn(i):
        rows = pl.ds(pl.multiple_of(i * 128, 128), 128)
        for h in range(4):
            at = 128 * h
            real, imag = whole[0, rows, at : at + 128].T, whole[1, rows, at : at + 128].T
            for k, part in enumerate((real, imag, real + imag)):
                high, low = halves(part)
                d[k, at : at + 128, rows] = high
                d[k, SIDE + at : SIDE + at + 128, rows] = low
                d[k, 2 * SIDE + at : 2 * SIDE + at + 128, rows] = high

    each(0, 4, turn)

    def multiply(left):
        one, two, three = (
            nn(jnp.concatenate([high, high, low], axis=1), d[k]) for k, (high, low) in enumerate(left))
        return one - two, three - one - two

    def band(i):
        rows = pl.ds(pl.multiple_of(i * BAND, BAND), BAND)
        lows = pl.ds(pl.multiple_of(SIDE + i * BAND, BAND), BAND)
        first = multiply([(d[k, rows, :], d[k, lows, :]) for k in range(3)])
        second = multiply([halves(v) for v in (first[0], first[1], first[0] + first[1])])
        for c in range(2):
            direct[c, rows, :] = gain[0, rows, :] * first[c] + gain[1, rows, :] * second[c]
            refl[2 * c, rows, :], refl[2 * c + 1, rows, :] = halves(
                mgain[0, rows, :] * first[c] + mgain[1, rows, :] * second[c])

    each(0, SIDE // BAND, band)
    for a in range(2):
        for b in range(2):
            ra, rb = slice(256 * a, 256 * a + 256), slice(256 * b, 256 * b + 256)
            for c in range(2):
                high = nt(ct[a], refl[2 * c, rb, ra]).astype(BF16)
                low = nt(ct[a], refl[2 * c + 1, rb, ra]).astype(BF16)
                total = direct[c, ra, rb] + (nn(high, ct[b]) + nn(low, ct[b]))
                for h in range(2):
                    both[c, h] = total[:, 128 * h : 128 * h + 128]

            def pack(i):
                for c in range(2):
                    for h in range(2):
                        outs = swap_groups(
                            [both[c, h, pl.ds(i * 64 + u, 16, stride=4), :] for u in range(4)], group)
                        for u in range(4):
                            send[4 * a + i, 8 * b + 4 * h + u, 16 * c : 16 * c + 16, :] = outs[u]

            each(0, 4, pack)

    pl.semaphore_wait(ready_sem, NP - 1)
    mine = pltpu.make_async_copy(send.at[p, q], recv.at[me], out_own)
    mine.start()
    for a, b, c in far_first(3):
        def put(e):
            dc, e = lax.rem(e, 2), e // 2
            dx, e = away(a, lax.rem(e, ways(a))), e // ways(a)
            dy, e = away(b, lax.rem(e, ways(b))), e // ways(b)
            dz = away(c, e)
            pp = lax.rem(z + dz, 4) * 2 + lax.rem(core + dc, 2)
            qq = lax.rem(x + dx, 4) * 4 + lax.rem(y + dy, 4)
            pltpu.make_async_remote_copy(
                send.at[pp, qq], recv.at[me], out_send, out_recv, device_id=(pp, qq), device_id_type=MESH).start()

        each(1 if a + b + c == 0 else 0, 2 * ways(a) * ways(b) * ways(c), put)
    each(1, 4, lambda t: slab(p, 0, t).wait_send())

    @pl.when(core == 1)
    def _():
        slab(p, 0, 0).wait_send()

    @pl.when(core == 0)
    def _():
        each(1, NP, lambda t: slab(0, 0, t + 3).wait_send())

    mine.wait()
    most = recv.at[pl.ds(0, NP * NQ - 1)]
    pltpu.make_async_copy(most, most, out_send).wait()
    pltpu.make_async_copy(most, most, out_recv).wait()


BAND = 256


def slot_work(spectra, gtile, prow, tab):
    dma = pltpu.SemaphoreType.DMA
    regular = pltpu.SemaphoreType.REGULAR
    return pl.pallas_call(
        slot_kernel,
        out_shape=jax.ShapeDtypeStruct((NP * NQ, 32, 128), F32),
        in_specs=[ANY, VMEM, VMEM, SMEM],
        out_specs=ANY,
        scratch_shapes=[
            pltpu.VMEM((2, SIDE, SIDE), F32),
            pltpu.VMEM((NP, NQ, 16, 128), jnp.int32),
            pltpu.VMEM((2, 256, 256), BF16),
            pltpu.VMEM((4, SIDE, 128), jnp.int32),
            pltpu.VMEM((SIDE, SIDE), jnp.int32),
            pltpu.VMEM((2, SIDE, SIDE), F32),
            pltpu.VMEM((2, SIDE, SIDE), F32),
            pltpu.VMEM((3, 3 * SIDE, SIDE), BF16),
            pltpu.VMEM((2, SIDE, SIDE), F32),
            pltpu.VMEM((4, SIDE, SIDE), BF16),
            pltpu.VMEM((2, 2, 256, 128), F32),
            pltpu.VMEM((NP, NQ, 32, 128), F32),
            dma((2,)), dma((NQ,)), dma((NQ,)), dma((NQ,)), dma((NQ,)), dma((11,)), dma((NP,)), regular, regular,
            dma, dma, dma,
        ],
        compiler_params=pltpu.CompilerParams(
            collective_id=0, has_side_effects=True, vmem_limit_bytes=48 << 20),
        name="slot_work",
    )(spectra, gtile, prow, tab)


PART = 8


def time_kernel(counts, recv, table, recorded, out, held, rec, res, fetch_sem, in_sem, out_sem):
    def load(i):
        at = pl.ds(i * PART, PART)
        return pltpu.make_async_copy(recorded.at[at], rec.at[at], in_sem.at[i])

    def store(i):
        at = pl.ds(i * PART, PART)
        return pltpu.make_async_copy(res.at[at], out.at[at], out_sem.at[i])

    parts = 64 // PART
    row = 0
    for p in range(NP):
        live = counts[p]

        def fetch(k):
            pltpu.make_async_copy(
                recv.at[p * NQ + k], held.at[pl.ds(pl.multiple_of((row + k) * 32, 32), 32), :], fetch_sem).start()

        each(0, live, fetch)
        row = row + live
    each(0, parts, lambda i: load(i).start())
    pltpu.make_async_copy(held, held, fetch_sem).wait()

    def part(i):
        load(i).wait()
        for k in range(PART // 4):
            j = i * (PART // 4) + k
            values = [held[pl.ds(c * 16 + j, LIVE, stride=32), :] for c in range(2)]
            high, low = halves(jnp.concatenate(values, axis=0).T)
            wave = nn(jnp.concatenate([high, low, high], axis=1), table[...])
            at = pl.ds(pl.multiple_of(4 * j, 4), 4)
            res[at] = rec[at] - wave.reshape(4, 32, NT)
        store(i).start()

    each(0, parts, part)
    each(0, parts, lambda i: store(i).wait())


def to_time(counts, recv, table, recorded):
    dma = pltpu.SemaphoreType.DMA
    return pl.pallas_call(
        time_kernel,
        out_shape=jax.ShapeDtypeStruct((64, 32, NT), F32),
        in_specs=[SMEM, ANY, VMEM, ANY],
        out_specs=ANY,
        scratch_shapes=[
            pltpu.VMEM((LIVE * 32, 128), F32),
            pltpu.VMEM((64, 32, NT), F32),
            pltpu.VMEM((64, 32, NT), F32),
            dma, dma((64 // PART,)), dma((64 // PART,)),
        ],
        name="to_time",
    )(counts, recv, table, recorded)


def on_device(spectra, counts, partner, recorded, gain_index, gain_table):
    gtile = gain_index.reshape(16, 128)
    recv = slot_work(spectra, gtile, partner.reshape(1, SIDE), gain_table)
    return to_time(counts, recv, jnp.asarray(basis()), recorded)


def solution(mesh):
    placed = (P("freq", None, "rcv", None), P(), P(), P("freq", "rcv", None), P("freq", "rcv"), P())
    return jax.shard_map(
        on_device, mesh=mesh, in_specs=placed, out_specs=P("freq", "rcv", None), check_vma=False
    )
```

profile of v0, /device:TPU:1, one launch (start us, length us, event | category | flops | bytes accessed | tf_op | source)
XLA Modules:
  0.0 85.1 jit_solution(17380725936763906295)
XLA Ops:
  0.0 0.8 copy.9
  0.8 0.1 reshape.6.gtile
  0.9 0.0 copy-start.1
  0.9 1.6 %copy-done.1 = f32[16,2,32,512]{3,2,1,0:T(8,128)S(1)} copy-done((f32[16,2,32,512]{3,2,1,0:T(8,128)S(1)}, f32[16,2,32,512]{3,2,1,0:T(8,128)}, u32[]{:S(2)}) %copy-start.1) | copy-done | bytes 2097176
  2.5 0.0 copy-start.2
  2.5 0.7 copy-done.2
  3.2 0.0 copy-start.3
  3.2 0.7 copy-done.3
  3.8 73.3 %slot_work.1.recv = f32[128,32,128]{2,1,0:T(8,128)S(1)} custom-call(f32[16,2,32,512]{3,2,1,0:T(8,128)S(1)} %copy-done.1, s32[16,128]{1,0:T(8,128)S(1)} %reshape.6.gtile, s32[1,512]{1,0:T(1,128)S(1)} %bitcast.1, f32[2,16]{1,0:T(2,128)S(1)} %copy-done.3), custom_call_target="tpu_custom_call" | custom-call | tf_op jit(solution)/shard_map/slot_work/pallas_call | solution.py:285
  77.1 0.0 copy-start
  77.1 1.3 %copy-done = f32[128,32,128]{2,1,0:T(8,128)} copy-done((f32[128,32,128]{2,1,0:T(8,128)}, f32[128,32,128]{2,1,0:T(8,128)S(1)}, u32[]{:S(2)}) %copy-start) | copy-done | bytes 2097176
  78.4 6.7 %to_time.1 = f32[64,32,512]{2,1,0:T(8,128)} custom-call(s32[8]{0:T(128)} %counts.1, f32[128,32,128]{2,1,0:T(8,128)} %copy-done, bf16[384,512]{1,0:T(8,128)(2,1)} %constant.2.clone.table, f32[64,32,512]{2,1,0:T(8,128)} %recorded.1), custom_call_target="tpu_custom_call" | custom-call | tf_op jit(solution)/shard_map/to_time/pallas_call | solution.py:355
Async XLA Ops:
  0.9 1.6 %copy-start.1 = (f32[16,2,32,512]{3,2,1,0:T(8,128)S(1)}, f32[16,2,32,512]{3,2,1,0:T(8,128)}, u32[]{:S(2)}) copy-start(f32[16,2,32,512]{3,2,1,0:T(8,128)} %spec.1) | copy-start | bytes 6291460
  2.5 0.7 copy-start.2
  3.2 0.7 copy-start.3
  77.1 1.3 %copy-start = (f32[128,32,128]{2,1,0:T(8,128)}, f32[128,32,128]{2,1,0:T(8,128)S(1)}, u32[]{:S(2)}) copy-start(f32[128,32,128]{2,1,0:T(8,128)S(1)} %slot_work.1.recv) | copy-start | bytes 6291460
where the time goes:
time: 85.4 us; the launch traced here: 85.1 us
  Pallas kernels  80 us (94%)
  local copies, waits for them, and re-layouts  5.15 us (6%)
    pallas_call x1, Pallas kernels, slot_work(): pl.pallas_call(slot_kernel, out_shape=jax.ShapeDtypeStruct((NP * NQ, 32,...  73.3 us
    pallas_call x1, Pallas kernels, to_time(): pl.pallas_call(time_kernel, out_shape=jax.ShapeDtypeStruct((64, 32, NT),...  6.68 us
    unnamed x9, local copies, waits for them, and re-layouts  5.08 us

commit v1 on v0

--- a/solution.py
+++ b/solution.py
@@ -1,4 +1,5 @@
 import itertools
+import random
 
 import jax
 import jax.numpy as jnp
@@ -76,21 +77,19 @@
     lax.fori_loop(first, last, body, 0)
 
 
-def away(a, code):
-    return a + code * (4 - 2 * a)
-
-
-def ways(a):
-    return 2 if a == 1 else 1
-
-
-def far_first(ranges):
-    return sorted(itertools.product(range(3), repeat=ranges), key=lambda c: (-sum(c), c))
+def near(offset):
+    return sum(min(step, 4 - step) for step in offset[:3])
+
+
+def far_first(shape, seed):
+    offsets = [offset for offset in itertools.product(*map(range, shape)) if any(offset)]
+    random.Random(seed).shuffle(offsets)
+    return sorted(offsets, key=lambda offset: -near(offset))
 
 
 def slot_kernel(
-    spec, gtile, prow, tab, recv,
-    whole, gains, ct, index, mirror, gain, mgain, d, direct, refl, both, send,
+    spec, gindex, partner, table, recv,
+    gtile, prow, tab, whole, gains, ct, index, mirror, gain, mgain, d, direct, refl, both, send,
     own_sem, row_send, row_recv, tile_send, tile_recv, slab_send, slab_recv, turn_sem, ready_sem,
     out_own, out_send, out_recv,
 ):
@@ -110,10 +109,24 @@
 
     each(1, NQ, greet_q)
     each(1, NP, greet_p)
-    own_tile = pltpu.make_async_copy(gtile, gains.at[p, q], own_sem.at[0])
-    own_rows = pltpu.make_async_copy(spec.at[q], whole.at[:, pl.ds(pl.multiple_of(q * 32, 32), 32), :], own_sem.at[1])
-    own_tile.start()
+    small = [pltpu.make_async_copy(src, dst, own_sem.at[i + 1]) for i, (src, dst) in enumerate(
+        ((gindex, gtile), (partner, prow), (table, tab)))]
+    for copy in small:
+        copy.start()
+    own_rows = pltpu.make_async_copy(spec.at[q], whole.at[:, pl.ds(pl.multiple_of(q * 32, 32), 32), :], own_sem.at[0])
     own_rows.start()
+    small[0].wait()
+    lanes = lax.broadcasted_iota(jnp.int32, (128, 32), 0)
+    repeat = (lax.rem(lanes, 32) == lax.broadcasted_iota(jnp.int32, (128, 32), 1)).astype(BF16)
+    levels = nn(repeat, gtile[...].astype(F32).astype(BF16))
+    sources = lax.broadcasted_iota(jnp.int32, (128, 64), 1)
+    groups = lax.broadcasted_iota(jnp.int32, (128, 64), 0) // 32
+    levels = jnp.where(lax.rem(sources, 4) == groups, levels, 0.0).astype(BF16)
+    fours = lax.broadcasted_iota(jnp.int32, (16, 64), 1) // 4
+    fours = (fours == lax.broadcasted_iota(jnp.int32, (16, 64), 0)).astype(BF16)
+    gains[p, q] = nt(fours, levels).astype(jnp.int32)
+    small[1].wait()
+    small[2].wait()
     for b in range(2):
         rows = lax.broadcasted_iota(jnp.int32, (256, 256), 0) + 256 * b
         ct[b] = (rows == prow[:, 256 * b : 256 * b + 256]).astype(F32).T.astype(BF16)
@@ -121,13 +134,16 @@
     each(1, NP, lambda t: pl.semaphore_signal(
         ready_sem, inc=1, device_id=(lax.rem(p + t, NP), q), device_id_type=MESH))
 
+    def at_offset(dx, dy):
+        return lax.rem(x + dx, 4) * 4 + lax.rem(y + dy, 4)
+
     def tile(t):
         return pltpu.make_async_remote_copy(
-            gtile, gains.at[p, q], tile_send.at[t], tile_recv.at[t],
-            device_id=(p, lax.rem(q + t, NQ)), device_id_type=MESH)
+            gains.at[p, q], gains.at[p, q], tile_send.at[t], tile_recv.at[t],
+            device_id=(p, at_offset(t // 4, lax.rem(t, 4))), device_id_type=MESH)
 
     def row(t):
-        k = lax.rem(q + t, NQ)
+        k = at_offset(t // 4, lax.rem(t, 4))
         return pltpu.make_async_remote_copy(
             spec.at[k], whole.at[:, pl.ds(pl.multiple_of(q * 32, 32), 32), :], row_send.at[t], row_recv.at[t],
             device_id=(p, k), device_id_type=MESH)
@@ -139,11 +155,14 @@
 
     each(1, NQ, lambda t: tile(t).start())
 
+    def start_rows():
+        for dx, dy in far_first((4, 4), 0):
+            row(4 * dx + dy).start()
+
     @pl.when(core == 0)
     def _():
-        each(1, NQ, lambda t: row(t).start())
-
-    own_tile.wait()
+        start_rows()
+
     each(1, NQ, lambda t: tile(t).wait())
 
     each(1, 4, lambda t: slab(p, lax.rem(z + t, 4) * 2, t).start())
@@ -162,7 +181,7 @@
     @pl.when(core == 1)
     def _():
         pl.semaphore_wait(turn_sem, 1)
-        each(1, NQ, lambda t: row(t).start())
+        start_rows()
         each(1, NP, lambda t: slab(lax.rem(p + t, NP), 0, 0).wait_recv())
 
     group = lane_group()
@@ -248,18 +267,11 @@
     pl.semaphore_wait(ready_sem, NP - 1)
     mine = pltpu.make_async_copy(send.at[p, q], recv.at[me], out_own)
     mine.start()
-    for a, b, c in far_first(3):
-        def put(e):
-            dc, e = lax.rem(e, 2), e // 2
-            dx, e = away(a, lax.rem(e, ways(a))), e // ways(a)
-            dy, e = away(b, lax.rem(e, ways(b))), e // ways(b)
-            dz = away(c, e)
-            pp = lax.rem(z + dz, 4) * 2 + lax.rem(core + dc, 2)
-            qq = lax.rem(x + dx, 4) * 4 + lax.rem(y + dy, 4)
-            pltpu.make_async_remote_copy(
-                send.at[pp, qq], recv.at[me], out_send, out_recv, device_id=(pp, qq), device_id_type=MESH).start()
-
-        each(1 if a + b + c == 0 else 0, 2 * ways(a) * ways(b) * ways(c), put)
+    for dx, dy, dz, dc in far_first((4, 4, 4, 2), 2):
+        pp = lax.rem(z + dz, 4) * 2 + lax.rem(core + dc, 2)
+        qq = at_offset(dx, dy)
+        pltpu.make_async_remote_copy(
+            send.at[pp, qq], recv.at[me], out_send, out_recv, device_id=(pp, qq), device_id_type=MESH).start()
     each(1, 4, lambda t: slab(p, 0, t).wait_send())
 
     @pl.when(core == 1)
@@ -277,17 +289,21 @@
 
 
 BAND = 256
-
-
-def slot_work(spectra, gtile, prow, tab):
+K1_VMEM = 63 << 20
+
+
+def slot_work(spectra, gindex, partner, table):
     dma = pltpu.SemaphoreType.DMA
     regular = pltpu.SemaphoreType.REGULAR
     return pl.pallas_call(
         slot_kernel,
         out_shape=jax.ShapeDtypeStruct((NP * NQ, 32, 128), F32),
-        in_specs=[ANY, VMEM, VMEM, SMEM],
+        in_specs=[ANY, ANY, ANY, ANY],
         out_specs=ANY,
         scratch_shapes=[
+            pltpu.VMEM((32, 64), jnp.int32),
+            pltpu.VMEM((1, SIDE), jnp.int32),
+            pltpu.SMEM((2, 16), F32),
             pltpu.VMEM((2, SIDE, SIDE), F32),
             pltpu.VMEM((NP, NQ, 16, 128), jnp.int32),
             pltpu.VMEM((2, 256, 256), BF16),
@@ -300,13 +316,13 @@
             pltpu.VMEM((4, SIDE, SIDE), BF16),
             pltpu.VMEM((2, 2, 256, 128), F32),
             pltpu.VMEM((NP, NQ, 32, 128), F32),
-            dma((2,)), dma((NQ,)), dma((NQ,)), dma((NQ,)), dma((NQ,)), dma((11,)), dma((NP,)), regular, regular,
+            dma((4,)), dma((NQ,)), dma((NQ,)), dma((NQ,)), dma((NQ,)), dma((11,)), dma((NP,)), regular, regular,
             dma, dma, dma,
         ],
         compiler_params=pltpu.CompilerParams(
-            collective_id=0, has_side_effects=True, vmem_limit_bytes=48 << 20),
+            collective_id=0, has_side_effects=True, vmem_limit_bytes=K1_VMEM),
         name="slot_work",
-    )(spectra, gtile, prow, tab)
+    )(spectra, gindex, partner, table)
 
 
 PART = 8
@@ -368,8 +384,7 @@
 
 
 def on_device(spectra, counts, partner, recorded, gain_index, gain_table):
-    gtile = gain_index.reshape(16, 128)
-    recv = slot_work(spectra, gtile, partner.reshape(1, SIDE), gain_table)
+    recv = slot_work(spectra, gain_index.T, partner.reshape(1, SIDE), gain_table)
     return to_time(counts, recv, jnp.asarray(basis()), recorded)
 
 

time: 85.4 us -> 75.6 us (0.89)
  local copies, waits for them, and re-layouts: 5.15 us -> 0 us
  Pallas kernels: 80 us -> 75.4 us
    unnamed x9 -> x0, local copies, waits for them, and re-layouts: 5.08 us -> none
    pallas_call x1, Pallas kernels: 73.3 us -> 68.7 us  [slot_work(): pl.pallas_call(slot_kernel, out_shape=jax.ShapeDtypeStruct((NP * NQ, 32,...]
where the time goes in v1:
time: 75.6 us; the launch traced here: 75.4 us
  Pallas kernels  75.4 us (100%)
    pallas_call x1, Pallas kernels, slot_work(): pl.pallas_call(slot_kernel, out_shape=jax.ShapeDtypeStruct((NP * NQ, 32,...  68.7 us
    pallas_call x1, Pallas kernels, to_time(): pl.pallas_call(time_kernel, out_shape=jax.ShapeDtypeStruct((64, 32, NT),...  6.68 us

profile of v1, /device:TPU:1, one launch (start us, length us, event | category | flops | bytes accessed | tf_op | source)
XLA Modules:
  0.0 75.4 jit_solution(15903964551572545853)
XLA Ops:
  0.0 68.7 %slot_work.1.recv = f32[128,32,128]{2,1,0:T(8,128)} custom-call(f32[16,2,32,512]{3,2,1,0:T(8,128)} %spec.1, s32[32,64]{1,0:T(8,128)} %bitcast.2, s32[1,512]{1,0:T(1,128)} %bitcast.3, f32[2,16]{1,0:T(2,128)} %table.2), custom_call_target="tpu_custom_call" | custom-call | tf_op jit(solution)/shard_map/slot_work/pallas_call | solution.py:298
  68.7 6.7 %to_time.1 = f32[64,32,512]{2,1,0:T(8,128)} custom-call(s32[8]{0:T(128)} %counts.1, f32[128,32,128]{2,1,0:T(8,128)} %slot_work.1.recv, bf16[384,512]{1,0:T(8,128)(2,1)} %constant.2.clone.table, f32[64,32,512]{2,1,0:T(8,128)} %recorded.1), custom_call_target="tpu_custom_call" | custom-call | tf_op jit(solution)/shard_map/to_time/pallas_call | solution.py:371

commit v2 on v1

--- a/solution.py
+++ b/solution.py
@@ -42,15 +42,16 @@
 
 
 def swap_groups(blocks, group):
-    outs = []
-    for g in range(4):
-        out = blocks[g]
-        for u in range(4):
-            if u != g:
-                moved = pltpu.roll(blocks[u], (32 * (u - g)) % 128, 1)
-                out = jnp.where(group == u, moved, out)
-        outs.append(out)
-    return outs
+    for step in (2, 1):
+        upper = (group & step) != 0
+        swapped = list(blocks)
+        for i in range(4):
+            if not i & step:
+                low, high = blocks[i], blocks[i + step]
+                swapped[i] = jnp.where(upper, pltpu.roll(high, 32 * step, 1), low)
+                swapped[i + step] = jnp.where(upper, high, pltpu.roll(low, 128 - 32 * step, 1))
+        blocks = swapped
+    return blocks
 
 
 def nt(a, b):
@@ -207,7 +208,6 @@
                 gain[o, rows, 128 * h : 128 * h + 128] = look_up(index[h, rows, :], entries)
             mgain[o, rows, :] = look_up(mirror[rows, :], entries)
 
-    each(0, SIDE // 16, gains_of)
     own_rows.wait()
     each(1, NQ, lambda t: row(t).wait_recv())
 
@@ -236,6 +236,8 @@
     def band(i):
         rows = pl.ds(pl.multiple_of(i * BAND, BAND), BAND)
         lows = pl.ds(pl.multiple_of(SIDE + i * BAND, BAND), BAND)
+        for u in range(BAND // 16):
+            gains_of(i * (BAND // 16) + u)
         first = multiply([(d[k, rows, :], d[k, lows, :]) for k in range(3)])
         second = multiply([halves(v) for v in (first[0], first[1], first[0] + first[1])])
         for c in range(2):
@@ -252,17 +254,18 @@
                 low = nt(ct[a], refl[2 * c + 1, rb, ra]).astype(BF16)
                 total = direct[c, ra, rb] + (nn(high, ct[b]) + nn(low, ct[b]))
                 for h in range(2):
-                    both[c, h] = total[:, 128 * h : 128 * h + 128]
+                    both[2 * a + b, c, h] = total[:, 128 * h : 128 * h + 128]
 
             def pack(i):
                 for c in range(2):
                     for h in range(2):
                         outs = swap_groups(
-                            [both[c, h, pl.ds(i * 64 + u, 16, stride=4), :] for u in range(4)], group)
+                            [both[2 * a + b, c, h, pl.ds(i * 64 + u, 16, stride=4), :] for u in range(4)], group)
                         for u in range(4):
                             send[4 * a + i, 8 * b + 4 * h + u, 16 * c : 16 * c + 16, :] = outs[u]
 
-            each(0, 4, pack)
+            for i in range(4):
+                pack(i)
 
     pl.semaphore_wait(ready_sem, NP - 1)
     mine = pltpu.make_async_copy(send.at[p, q], recv.at[me], out_own)
@@ -288,7 +291,7 @@
     pltpu.make_async_copy(most, most, out_recv).wait()
 
 
-BAND = 256
+BAND = 128
 K1_VMEM = 63 << 20
 
 
@@ -314,7 +317,7 @@
             pltpu.VMEM((3, 3 * SIDE, SIDE), BF16),
             pltpu.VMEM((2, SIDE, SIDE), F32),
             pltpu.VMEM((4, SIDE, SIDE), BF16),
-            pltpu.VMEM((2, 2, 256, 128), F32),
+            pltpu.VMEM((4, 2, 2, 256, 128), F32),
             pltpu.VMEM((NP, NQ, 32, 128), F32),
             dma((4,)), dma((NQ,)), dma((NQ,)), dma((NQ,)), dma((NQ,)), dma((11,)), dma((NP,)), regular, regular,
             dma, dma, dma,
@@ -325,10 +328,10 @@
     )(spectra, gindex, partner, table)
 
 
-PART = 8
-
-
-def time_kernel(counts, recv, table, recorded, out, held, rec, res, fetch_sem, in_sem, out_sem):
+PART = 16
+
+
+def time_kernel(counts, recv, table, recorded, out, held, wave_table, rec, res, fetch_sem, table_sem, in_sem, out_sem):
     def load(i):
         at = pl.ds(i * PART, PART)
         return pltpu.make_async_copy(recorded.at[at], rec.at[at], in_sem.at[i])
@@ -348,18 +351,23 @@
 
         each(0, live, fetch)
         row = row + live
+    basis_copy = pltpu.make_async_copy(table, wave_table, table_sem)
+    basis_copy.start()
     each(0, parts, lambda i: load(i).start())
+    basis_copy.wait()
     pltpu.make_async_copy(held, held, fetch_sem).wait()
 
     def part(i):
         load(i).wait()
+        chunks = []
         for k in range(PART // 4):
             j = i * (PART // 4) + k
             values = [held[pl.ds(c * 16 + j, LIVE, stride=32), :] for c in range(2)]
-            high, low = halves(jnp.concatenate(values, axis=0).T)
-            wave = nn(jnp.concatenate([high, low, high], axis=1), table[...])
-            at = pl.ds(pl.multiple_of(4 * j, 4), 4)
-            res[at] = rec[at] - wave.reshape(4, 32, NT)
+            chunks.append(jnp.concatenate(values, axis=0).T)
+        high, low = halves(jnp.concatenate(chunks, axis=0))
+        wave = nn(jnp.concatenate([high, low, high], axis=1), wave_table[...])
+        at = pl.ds(pl.multiple_of(i * PART, PART), PART)
+        res[at] = rec[at] - wave.reshape(PART, 32, NT)
         store(i).start()
 
     each(0, parts, part)
@@ -371,13 +379,14 @@
     return pl.pallas_call(
         time_kernel,
         out_shape=jax.ShapeDtypeStruct((64, 32, NT), F32),
-        in_specs=[SMEM, ANY, VMEM, ANY],
+        in_specs=[SMEM, ANY, ANY, ANY],
         out_specs=ANY,
         scratch_shapes=[
             pltpu.VMEM((LIVE * 32, 128), F32),
+            pltpu.VMEM((6 * LIVE, NT), BF16),
             pltpu.VMEM((64, 32, NT), F32),
             pltpu.VMEM((64, 32, NT), F32),
-            dma, dma((64 // PART,)), dma((64 // PART,)),
+            dma, dma, dma((64 // PART,)), dma((64 // PART,)),
         ],
         name="to_time",
     )(counts, recv, table, recorded)

time: 75.6 us -> 70.8 us (0.937)
  Pallas kernels: 75.4 us -> 70.7 us
    pallas_call x1, Pallas kernels: 68.7 us -> 64.8 us  [slot_work(): pl.pallas_call(slot_kernel, out_shape=jax.ShapeDtypeStruct((NP * NQ, 32,...]
    pallas_call x1, Pallas kernels: 6.68 us -> 5.91 us  [to_time(): pl.pallas_call(time_kernel, out_shape=jax.ShapeDtypeStruct((64, 32, NT),...]
where the time goes in v2:
time: 70.8 us; the launch traced here: 70.7 us
  Pallas kernels  70.7 us (100%)
    pallas_call x1, Pallas kernels, slot_work(): pl.pallas_call(slot_kernel, out_shape=jax.ShapeDtypeStruct((NP * NQ, 32,...  64.8 us
    pallas_call x1, Pallas kernels, to_time(): pl.pallas_call(time_kernel, out_shape=jax.ShapeDtypeStruct((64, 32, NT),...  5.91 us

profile of v2, /device:TPU:1, one launch (start us, length us, event | category | flops | bytes accessed | tf_op | source)
XLA Modules:
  0.0 70.7 jit_solution(16973254301323713583)
XLA Ops:
  0.0 64.8 %slot_work.1.recv = f32[128,32,128]{2,1,0:T(8,128)} custom-call(f32[16,2,32,512]{3,2,1,0:T(8,128)} %spec.1, s32[32,64]{1,0:T(8,128)} %bitcast.2, s32[1,512]{1,0:T(1,128)} %bitcast.3, f32[2,16]{1,0:T(2,128)} %table.2), custom_call_target="tpu_custom_call" | custom-call | tf_op jit(solution)/shard_map/slot_work/pallas_call | solution.py:301
  64.8 5.9 %to_time.1 = f32[64,32,512]{2,1,0:T(8,128)} custom-call(s32[8]{0:T(128)} %counts.1, f32[128,32,128]{2,1,0:T(8,128)} %slot_work.1.recv, bf16[384,512]{1,0:T(8,128)(2,1)} %constant.2.clone.table, f32[64,32,512]{2,1,0:T(8,128)} %recorded.1), custom_call_target="tpu_custom_call" | custom-call | tf_op jit(solution)/shard_map/to_time/pallas_call | solution.py:379

commit v3 on v2

--- a/solution.py
+++ b/solution.py
@@ -176,8 +176,11 @@
     def _():
         each(1, NP, lambda t: slab(lax.rem(p + t, NP), 0, 0).wait_recv())
         each(1, NP, lambda t: slab(lax.rem(p + 1 + t, NP), p + 1, t + 3).start())
-        each(1, NQ, lambda t: row(t).wait_send())
+        for dx, dy in far_first((4, 4), 0)[:12]:
+            row(4 * dx + dy).wait_send()
         pl.semaphore_signal(turn_sem, inc=1, device_id=(p + 1, q), device_id_type=MESH)
+        for dx, dy in far_first((4, 4), 0)[12:]:
+            row(4 * dx + dy).wait_send()
 
     @pl.when(core == 1)
     def _():
@@ -216,7 +219,7 @@
         each(1, NQ, lambda t: row(t).wait_send())
 
     def turn(i):
-        rows = pl.ds(pl.multiple_of(i * 128, 128), 128)
+        rows = pl.ds(128 * i, 128)
         for h in range(4):
             at = 128 * h
             real, imag = whole[0, rows, at : at + 128].T, whole[1, rows, at : at + 128].T
@@ -226,7 +229,8 @@
                 d[k, SIDE + at : SIDE + at + 128, rows] = low
                 d[k, 2 * SIDE + at : 2 * SIDE + at + 128, rows] = high
 
-    each(0, 4, turn)
+    for i in range(4):
+        turn(i)
 
     def multiply(left):
         one, two, three = (
@@ -345,11 +349,9 @@
     for p in range(NP):
         live = counts[p]
 
-        def fetch(k):
-            pltpu.make_async_copy(
-                recv.at[p * NQ + k], held.at[pl.ds(pl.multiple_of((row + k) * 32, 32), 32), :], fetch_sem).start()
-
-        each(0, live, fetch)
+        pltpu.make_async_copy(
+            recv.at[pl.ds(p * NQ * 32, live * 32), :],
+            held.at[pl.ds(pl.multiple_of(row * 32, 32), live * 32), :], fetch_sem).start()
         row = row + live
     basis_copy = pltpu.make_async_copy(table, wave_table, table_sem)
     basis_copy.start()
@@ -389,7 +391,7 @@
             dma, dma, dma((64 // PART,)), dma((64 // PART,)),
         ],
         name="to_time",
-    )(counts, recv, table, recorded)
+    )(counts, recv.reshape(NP * NQ * 32, 128), table, recorded)
 
 
 def on_device(spectra, counts, partner, recorded, gain_index, gain_table):

time: 70.8 us -> 70 us (0.989)
  Pallas kernels: 70.7 us -> 69.8 us
where the time goes in v3:
time: 70 us; the launch traced here: 69.8 us
  Pallas kernels  69.8 us (100%)
    pallas_call x1, Pallas kernels, slot_work(): pl.pallas_call(slot_kernel, out_shape=jax.ShapeDtypeStruct((NP * NQ, 32,...  64.2 us
    pallas_call x1, Pallas kernels, to_time(): pl.pallas_call(time_kernel, out_shape=jax.ShapeDtypeStruct((64, 32, NT),...  5.62 us

profile of v3, /device:TPU:1, one launch (start us, length us, event | category | flops | bytes accessed | tf_op | source)
XLA Modules:
  0.0 69.8 jit_solution(16450393391704054794)
XLA Ops:
  0.0 64.2 %slot_work.1 = f32[128,32,128]{2,1,0:T(8,128)} custom-call(f32[16,2,32,512]{3,2,1,0:T(8,128)} %spec.1, s32[32,64]{1,0:T(8,128)} %bitcast.4, s32[1,512]{1,0:T(1,128)} %bitcast.5, f32[2,16]{1,0:T(2,128)} %table.2), custom_call_target="tpu_custom_call" | custom-call | tf_op jit(solution)/shard_map/slot_work/pallas_call | solution.py:305
  64.2 5.6 %to_time.1 = f32[64,32,512]{2,1,0:T(8,128)} custom-call(s32[8]{0:T(128)} %counts.1, f32[4096,128]{1,0:T(8,128)} %bitcast.3, bf16[384,512]{1,0:T(8,128)(2,1)} %constant.2.clone.table, f32[64,32,512]{2,1,0:T(8,128)} %recorded.1), custom_call_target="tpu_custom_call" | custom-call | tf_op jit(solution)/shard_map/to_time/pallas_call | solution.py:381

commit v4 on v3

--- a/solution.py
+++ b/solution.py
@@ -274,7 +274,7 @@
     pl.semaphore_wait(ready_sem, NP - 1)
     mine = pltpu.make_async_copy(send.at[p, q], recv.at[me], out_own)
     mine.start()
-    for dx, dy, dz, dc in far_first((4, 4, 4, 2), 2):
+    for dx, dy, dz, dc in far_first((4, 4, 4, 2), 9):
         pp = lax.rem(z + dz, 4) * 2 + lax.rem(core + dc, 2)
         qq = at_offset(dx, dy)
         pltpu.make_async_remote_copy(
@@ -368,11 +368,12 @@
             chunks.append(jnp.concatenate(values, axis=0).T)
         high, low = halves(jnp.concatenate(chunks, axis=0))
         wave = nn(jnp.concatenate([high, low, high], axis=1), wave_table[...])
-        at = pl.ds(pl.multiple_of(i * PART, PART), PART)
+        at = pl.ds(i * PART, PART)
         res[at] = rec[at] - wave.reshape(PART, 32, NT)
         store(i).start()
 
-    each(0, parts, part)
+    for i in range(parts):
+        part(i)
     each(0, parts, lambda i: store(i).wait())
 
 

time: 70 us -> 69.9 us (level)
  no operation moved by 1% of the time
where the time goes in v4:
time: 69.9 us; the launch traced here: 69.7 us
  Pallas kernels  69.7 us (100%)
    pallas_call x1, Pallas kernels, slot_work(): pl.pallas_call(slot_kernel, out_shape=jax.ShapeDtypeStruct((NP * NQ, 32,...  64 us
    pallas_call x1, Pallas kernels, to_time(): pl.pallas_call(time_kernel, out_shape=jax.ShapeDtypeStruct((64, 32, NT),...  5.64 us

profile of v4, /device:TPU:1, one launch (start us, length us, event | category | flops | bytes accessed | tf_op | source)
XLA Modules:
  0.0 69.7 jit_solution(11540910272866066361)
XLA Ops:
  0.0 64.0 %slot_work.1 = f32[128,32,128]{2,1,0:T(8,128)} custom-call(f32[16,2,32,512]{3,2,1,0:T(8,128)} %spec.1, s32[32,64]{1,0:T(8,128)} %bitcast.4, s32[1,512]{1,0:T(1,128)} %bitcast.5, f32[2,16]{1,0:T(2,128)} %table.2), custom_call_target="tpu_custom_call" | custom-call | tf_op jit(solution)/shard_map/slot_work/pallas_call | solution.py:305
  64.0 5.6 %to_time.1 = f32[64,32,512]{2,1,0:T(8,128)} custom-call(s32[8]{0:T(128)} %counts.1, f32[4096,128]{1,0:T(8,128)} %bitcast.3, bf16[384,512]{1,0:T(8,128)(2,1)} %constant.2.clone.table, f32[64,32,512]{2,1,0:T(8,128)} %recorded.1), custom_call_target="tpu_custom_call" | custom-call | tf_op jit(solution)/shard_map/to_time/pallas_call | solution.py:382
